TPU v7x, 512 devices: a whole 4x4x16 slice. The times are simulated.
512 devices in a mesh: gx: 8 (over z_lo), gy: 8 (over y, z_hi), gz: 8 (over x, core).
Axes of the slice: x: 4, y: 4, z: 16 (z_hi: 2, z_lo: 8; z = z_hi * 8 + z_lo), core: 2. Of those that a mesh axis runs over, the one named last changes fastest.
Arguments:
- state_send: float32 [13, 216, 65536], P(None, None, ('gx', 'gy', 'gz')), may hold values from -0.5 to 14, as said below
- order_send: int32 [65536], P(('gx', 'gy', 'gz')), may hold values from 1 to 5
- send_count: int32 [512, 64], P(('gx', 'gy', 'gz')), may hold values from 0 to 2, as said below
- neighbours: int32 [6, 65536], P(None, ('gx', 'gy', 'gz')), may hold values from 0 to 159, as said below
Outputs:
- new_state: float32 [13, 216, 65536], P(None, None, ('gx', 'gy', 'gz'))
Inputs may be any that keep to these rules, and one draw needn't show every extreme that they name: `state_send`: rows 0 to 8 are species densities in [0.005, 2], rows 9 to 11 momenta in [-0.5, 0.5], row 12 total energy in [3, 14], with energy above 0.5 |momentum|^2 / density at every node. `send_count`: in every draw one receiver of each gx index gets 2 elements from every device of that index. `neighbours`: every face of a live new element names a live element; faces 0, 2, 4 of slots below 16 may name the previous device's last 16 slots, faces 1, 3, 5 of the last 16 slots the next device's first 16; the first device has no previous and the last no next; empty slots name themselves.
All inputs are finite; a program needn't handle non-finite values.
Results may differ from a plain program's by a relative error of at most 0.0003.
Values sent between devices are 32-bit elements; how exact they have to be, the bound alone decides.
No kernel may reach another device: no remote copies, remote signals or barrier semaphores. Data moves between devices by JAX's collectives and lax.ppermute only.
A program may use at most 128 MiB of HBM per device.

v0:
```python
import jax
import jax.numpy as jnp
import numpy as np
from jax import lax
from jax.sharding import PartitionSpec as P

NV = 13
PMAX = 5
NODES = 216
BAND = 16
step_scale = 0.02
positivity_eps = 0.001
floor_gap = 0.05


def padded(value, sides, width):
    for axis, dim in sides:
        count, length = (lax.axis_size(axis), value.shape[dim])
        up = [(i, (i + 1) % count) for i in range(count - 1)]
        down = [(j, i) for i, j in up]
        last = lax.slice_in_dim(value, length - width, length, axis=dim)
        initial = lax.slice_in_dim(value, 0, width, axis=dim)
        before = lax.ppermute(last, axis, up)
        after = lax.ppermute(initial, axis, down)
        value = jnp.concatenate([before, value, after], axis=dim)
    return value


def lagrange_coeffs(node_pos, column):
    coeffs = [1.0]
    denom = 1.0
    for other in range(len(node_pos)):
        if other == column:
            continue
        shifted = [0.0] * (len(coeffs) + 1)
        for power in range(len(coeffs)):
            shifted[power + 1] += coeffs[power]
            shifted[power] -= float(node_pos[other]) * coeffs[power]
        coeffs = shifted
        denom = denom * (float(node_pos[column]) - float(node_pos[other]))
    return [value / denom for value in coeffs]


def poly_value(coeffs, point):
    total = 0.0
    for power in range(len(coeffs)):
        total += coeffs[power] * point**power
    return total


def poly_slope(coeffs, point):
    total = 0.0
    for power in range(1, len(coeffs)):
        total += power * coeffs[power] * point ** (power - 1)
    return total


def poly_integral(coeffs):
    total = 0.0
    for power in range(len(coeffs)):
        total += coeffs[power] * (1.0 - (-1.0) ** (power + 1)) / (power + 1)
    return total


def basis_tables():
    points = PMAX + 1
    common = np.linspace(-1.0, 1.0, points)
    derivs = np.zeros((PMAX, points, points))
    weights = np.zeros((PMAX, points))
    inverse = np.zeros((PMAX, points))
    interp = np.zeros((PMAX, points, points))
    for degree in range(1, PMAX + 1):
        node_pos = np.linspace(-1.0, 1.0, degree + 1)
        for column in range(degree + 1):
            coeffs = lagrange_coeffs(node_pos, column)
            weights[degree - 1, column] = poly_integral(coeffs)
            for row in range(points):
                interp[degree - 1, row, column] = poly_value(coeffs, float(common[row]))
            for row in range(degree + 1):
                derivs[degree - 1, row, column] = poly_slope(coeffs, float(node_pos[row]))
        inverse[degree - 1, : degree + 1] = 1.0 / weights[degree - 1, : degree + 1]
    return (derivs, weights, inverse, interp, weights[PMAX - 1].copy())


def selections(degree):
    points = PMAX + 1
    derivs, weights, inverse, interp, common_w = basis_tables()
    highest = lax.Precision.HIGHEST
    levels = jnp.arange(1, PMAX + 1, dtype=jnp.int32)
    onehot = (degree[None, :] == levels[:, None]).astype(jnp.float32)
    deriv_sel = jnp.einsum(
        "pij,pe->ije", jnp.asarray(derivs, jnp.float32), onehot, precision=highest
    )
    weight_sel = jnp.einsum(
        "pi,pe->ie", jnp.asarray(weights, jnp.float32), onehot, precision=highest
    )
    inverse_sel = jnp.einsum(
        "pi,pe->ie", jnp.asarray(inverse, jnp.float32), onehot, precision=highest
    )
    interp_sel = jnp.einsum(
        "pqj,pe->qje", jnp.asarray(interp, jnp.float32), onehot, precision=highest
    )
    weighted_interp = interp_sel * jnp.asarray(common_w, jnp.float32)[:, None, None]
    positions = jnp.arange(points, dtype=jnp.int32)[:, None]
    is_live = degree[None, :] > 0
    active = ((positions <= degree[None, :]) & is_live).astype(jnp.float32)
    low_sel = ((positions == 0) & is_live).astype(jnp.float32)
    high_sel = ((positions == degree[None, :]) & is_live).astype(jnp.float32)
    return (
        deriv_sel,
        weight_sel,
        inverse_sel,
        interp_sel,
        weighted_interp,
        active,
        low_sel,
        high_sel,
    )


def apply_along(matrix, data, axis):
    total = None
    for column in range(matrix.shape[1]):
        piece = lax.index_in_dim(data, column, axis, keepdims=True)
        shape = [1] * data.ndim
        shape[axis] = matrix.shape[0]
        shape[-1] = matrix.shape[-1]
        term = matrix[:, column, :].reshape(shape) * piece
        total = term if total is None else total + term
    return total


def pick_layer(selector, data, axis):
    total = None
    for row in range(selector.shape[0]):
        piece = lax.index_in_dim(data, row, axis, keepdims=False)
        shape = [1] * piece.ndim
        shape[-1] = selector.shape[-1]
        term = selector[row].reshape(shape) * piece
        total = term if total is None else total + term
    return total


def place_layer(selector, layer, axis):
    expanded = jnp.expand_dims(layer, axis)
    shape = [1] * expanded.ndim
    shape[axis] = selector.shape[0]
    shape[-1] = selector.shape[-1]
    return selector.reshape(shape) * expanded


def element_terms(state_rows, setup):
    deriv_sel, weight_sel, inverse_sel, interp_sel, weighted_interp, active, low_sel, high_sel = (
        setup
    )
    points = PMAX + 1
    slot_count = state_rows.shape[-1]
    node_mask = active[:, None, None, :] * active[None, :, None, :] * active[None, None, :, :]
    field = state_rows.reshape(NV, points, points, points, slot_count) * node_mask[None]
    species = field[:9]
    momentum = field[9:12]
    energy = field[12]
    density = jnp.sum(species, axis=0)
    safe_rho = jnp.where(node_mask > 0, density, 1.0)
    velocity = momentum / safe_rho[None]
    pressure = 0.4 * (energy - 0.5 * jnp.sum(momentum * velocity, axis=0))
    sound_speed = jnp.sqrt(1.4 * jnp.where(node_mask > 0, pressure, 1.0) / safe_rho)
    volume = jnp.zeros_like(field)
    face_list = []
    for axis_pos in range(3):
        normal_vel = velocity[axis_pos]
        unit = jnp.eye(3, dtype=jnp.float32)[axis_pos].reshape(3, 1, 1, 1, 1)
        flux_dim = (
            jnp.concatenate(
                [
                    species * normal_vel[None],
                    momentum * normal_vel[None] + pressure[None] * unit,
                    ((energy + pressure) * normal_vel)[None],
                ],
                axis=0,
            )
            * node_mask[None]
        )
        speeds = (jnp.abs(normal_vel) + sound_speed) * node_mask
        volume = volume + apply_along(deriv_sel, flux_dim, axis_pos + 1)
        for face_side in range(2):
            selector = low_sel if face_side == 0 else high_sel
            normal_sign = -1.0 if face_side == 0 else 1.0
            u_face = pick_layer(selector, field, axis_pos + 1)
            g_face = normal_sign * pick_layer(selector, flux_dim, axis_pos + 1)
            s_face = pick_layer(selector, speeds, axis_pos)
            face_speed = jnp.max(s_face, axis=(0, 1))
            u_common = apply_along(interp_sel, apply_along(interp_sel, u_face, 1), 2)
            g_common = apply_along(interp_sel, apply_along(interp_sel, g_face, 1), 2)
            face_rows = jnp.concatenate(
                [
                    u_common.reshape(NV, points * points, slot_count),
                    g_common.reshape(NV, points * points, slot_count),
                    jnp.broadcast_to(face_speed[None, None, :], (1, points * points, slot_count)),
                ],
                axis=0,
            )
            face_list.append(face_rows)
    traces = jnp.stack(face_list, axis=1)
    return (field, volume, traces, node_mask)


def finish(field, volume, traces, extended, links, setup, node_mask):
    deriv_sel, weight_sel, inverse_sel, interp_sel, weighted_interp, active, low_sel, high_sel = (
        setup
    )
    points = PMAX + 1
    slot_count = field.shape[-1]
    lift_table = weighted_interp.transpose(1, 0, 2)
    surface = jnp.zeros_like(field)
    for face in range(6):
        axis_pos = face // 2
        selector = low_sel if face % 2 == 0 else high_sel
        own_rows = traces[:, face]
        far_rows = jnp.take(extended[:, face ^ 1], links[face], axis=-1)
        penalty = jnp.maximum(own_rows[2 * NV], far_rows[2 * NV])
        jump_flux = 0.5 * (-far_rows[NV : 2 * NV] - own_rows[NV : 2 * NV]) - 0.5 * penalty[None] * (
            far_rows[:NV] - own_rows[:NV]
        )
        jump_flux = jump_flux.reshape(NV, points, points, slot_count)
        inv_face = jnp.sum(selector * inverse_sel, axis=0)
        lifted = apply_along(lift_table, apply_along(lift_table, jump_flux, 1), 2)
        lifted = lifted * (
            inverse_sel[None, :, None, :]
            * inverse_sel[None, None, :, :]
            * inv_face[None, None, None, :]
        )
        surface = surface + place_layer(selector, lifted, axis_pos + 1)
    section = (field - step_scale * (volume + surface)) * node_mask[None]
    node_weight = (
        weight_sel[:, None, None, :]
        * weight_sel[None, :, None, :]
        * weight_sel[None, None, :, :]
        / 8.0
    )
    species = section[:9]
    average = jnp.sum(species * node_weight[None], axis=(1, 2, 3))
    lowest = jnp.min(jnp.where(node_mask[None] > 0, species, 1e30), axis=(1, 2, 3))
    scaling = jnp.minimum(
        1.0, jnp.maximum(average - positivity_eps, 0.0) / jnp.maximum(average - lowest, floor_gap)
    )
    scaled = (
        average[:, None, None, None, :]
        + scaling[:, None, None, None, :] * (species - average[:, None, None, None, :])
    ) * node_mask[None]
    return jnp.concatenate([scaled, section[9:]], axis=0).reshape(NV, NODES, slot_count)


def local(state_send, order_send, send_count, neighbours):
    slot_count = state_send.shape[-1]
    peer_count = lax.axis_size(("gy", "gz"))
    capacity = slot_count // peer_count
    positions = jnp.arange(slot_count, dtype=jnp.int32)
    per_slot = jnp.broadcast_to(send_count.reshape(peer_count, 1), (peer_count, capacity)).reshape(
        slot_count
    )
    live_send = positions % capacity < per_slot
    order_tags = jnp.where(live_send, order_send, 0).astype(jnp.float32).reshape(1, 1, slot_count)
    moved, tags_in = (
        lax.all_to_all(state_send, ("gy", "gz"), split_axis=2, concat_axis=2, tiled=True),
        lax.all_to_all(order_tags, ("gy", "gz"), split_axis=2, concat_axis=2, tiled=True),
    )
    degree = tags_in.reshape(slot_count).astype(jnp.int32)
    setup = selections(degree)
    field, volume, traces, node_mask = element_terms(moved, setup)
    extended = padded(traces, ((("gx", "gy", "gz"), 3),), BAND)
    return finish(field, volume, traces, extended, neighbours, setup, node_mask)


def solution(mesh):
    placed = (
        P(None, None, ("gx", "gy", "gz")),
        P(("gx", "gy", "gz")),
        P(("gx", "gy", "gz"), None),
        P(None, ("gx", "gy", "gz")),
    )
    return jax.shard_map(
        local,
        mesh=mesh,
        in_specs=placed,
        out_specs=P(None, None, ("gx", "gy", "gz")),
        check_vma=False,
    )
```

profile of v0, /device:TPU:32, one launch (start us, length us, event | category | flops | bytes accessed | tf_op | source)
XLA Modules:
  0.0 377.1 jit_solution(7790423187221642835)
XLA Ops:
  2.3 20.3 %all-to-all-start.1 = ((f32[1,1,128]{1,0,2:T(1,128)}), f32[1,1,128]{1,0,2:T(1,128)S(1)}, u32[]{:S(2)}, u32[]{:S(2)}) async-start(f32[1,1,128]{1,0,2:T(1,128)} %copy.2597), calls=%async_computation.1 | async-start | bytes 131072 | tf_op jit(solution)/shard_map/all_to_all | solution.py:266
  25.3 3.0 copy.2595
  28.3 11.0 %all-to-all-done.1 = f32[1,1,128]{1,0,2:T(1,128)S(1)} async-done(((f32[1,1,128]{1,0,2:T(1,128)}), f32[1,1,128]{1,0,2:T(1,128)S(1)}, u32[]{:S(2)}, u32[]{:S(2)}) %all-to-all-start.1) | async-done | bytes 544 | tf_op jit(solution)/shard_map/all_to_all | solution.py:266
  39.3 6.7 %all-to-all-start = ((f32[13,216,128]{1,0,2:T(8,128)}), f32[13,216,128]{1,0,2:T(8,128)S(1)}, u32[]{:S(2)}, u32[]{:S(2)}) async-start(f32[13,216,128]{1,0,2:T(8,128)} %copy.2595), calls=%async_computation | async-start | bytes 4194304 | tf_op jit(solution)/shard_map/all_to_all | solution.py:265
  47.3 2.4 convert_reduce_fusion
  61.4 89.4 %all-to-all-done = f32[13,216,128]{1,0,2:T(8,128)S(1)} async-done(((f32[13,216,128]{1,0,2:T(8,128)}), f32[13,216,128]{1,0,2:T(8,128)S(1)}, u32[]{:S(2)}, u32[]{:S(2)}) %all-to-all-start) | async-done | bytes 1437728 | tf_op jit(solution)/shard_map/all_to_all | solution.py:265
  177.8 3.9 %fusion.139 = (f32[27,6,36,16]{3,2,0,1:T(8,128)}, f32[27,6,36,16]{3,2,0,1:T(8,128)}) fusion(f32[27,6,36,128]{3,2,0,1:T(8,128)S(1)} %fusion.5), kind=kLoop, calls=%fused_computation.678 | loop fusion | bytes 1492992 | tf_op jit(solution)/shard_map/slice | solution.py:21
  181.6 3.5 copy.2746
  185.2 2.4 collective-permute-start
  187.6 3.5 copy.2747
  191.1 15.3 %collective-permute-start.1 = (f32[27,6,36,16]{2,3,1,0:T(8,128)}, f32[27,6,36,16]{2,3,1,0:T(8,128)}, u32[]{:S(2)}, u32[]{:S(2)}) collective-permute-start(f32[27,6,36,16]{2,3,1,0:T(8,128)} %copy.2747), channel_id=1, source_target_pairs={{1,0},{2,1},{3,2},{4,3},{5,4},{6,5},{7,6},{8,7},{9,8},{10,9},{11,1... | collective-permute-start | bytes 1119752 | tf_op jit(solution)/shard_map/ppermute | solution.py:24
  215.2 62.9 %collective-permute-done = f32[27,6,36,16]{2,3,1,0:T(8,128)} collective-permute-done((f32[27,6,36,16]{2,3,1,0:T(8,128)}, f32[27,6,36,16]{2,3,1,0:T(8,128)}, u32[]{:S(2)}, u32[]{:S(2)}) %collective-permute-start) | collective-permute-done | bytes 373280 | tf_op jit(solution)/shard_map/ppermute | solution.py:23
  278.1 4.0 %copy.2748 = f32[27,6,36,16]{3,2,0,1:T(8,128)} copy(f32[27,6,36,16]{2,3,1,0:T(8,128)} %collective-permute-done) | data formatting | bytes 746496 | tf_op jit(solution)/shard_map/ppermute | solution.py:23
  282.1 3.6 copy.2749
  285.7 5.6 %pad_maximum_fusion = f32[27,6,36,160]{3,2,0,1:T(8,128)S(1)} fusion(f32[27,6,36,16]{3,2,0,1:T(8,128)} %copy.2749, f32[27,6,36,128]{3,2,0,1:T(8,128)S(1)} %fusion.5, f32[27,6,36,16]{3,2,0,1:T(8,128)} %copy.2748), kind=kLoop, calls=%fused_computation.6 | loop fusion | flops 1866240 | bytes 7464960 | tf_op jit(solution)/shard_map/concatenate | solution.py:25
  293.3 3.4 copy.2762
  296.7 3.9 %gather_fusion.3 = f32[128,27,36]{2,1,0:T(8,128)} fusion(f32[27,36,160]{1,0,2:T(8,128)} %copy.2762, s32[1024]{0:T(1024)} %get-tuple-element.415), kind=kCustom, calls=%fused_computation.3.clone | custom fusion | bytes 995840 | tf_op jit(solution)/shard_map/jit(_take)/gather | solution.py:220
  300.5 3.3 copy.2763
  306.8 3.4 copy.2758
  310.2 3.9 %gather_fusion.2 = f32[128,27,36]{2,1,0:T(8,128)} fusion(f32[27,36,160]{1,0,2:T(8,128)} %copy.2758, s32[1024]{0:T(1024)} %get-tuple-element.416), kind=kCustom, calls=%fused_computation.2.clone | custom fusion | bytes 995840 | tf_op jit(solution)/shard_map/jit(_take)/gather | solution.py:220
  314.1 3.3 copy.2759
  321.6 3.4 copy.2754
  325.0 3.9 %gather_fusion.1 = f32[128,27,36]{2,1,0:T(8,128)} fusion(f32[27,36,160]{1,0,2:T(8,128)} %copy.2754, s32[1024]{0:T(1024)} %get-tuple-element.417), kind=kCustom, calls=%fused_computation.1.clone | custom fusion | bytes 995840 | tf_op jit(solution)/shard_map/jit(_take)/gather | solution.py:220
  328.9 3.3 copy.2755
  335.2 2.6 copy.2750
  337.7 3.9 %gather_fusion = f32[128,27,36]{2,1,0:T(8,128)} fusion(f32[27,36,160]{1,0,2:T(8,128)} %copy.2750, s32[1024]{0:T(1024)} %get-tuple-element.418), kind=kCustom, calls=%fused_computation.clone | custom fusion | bytes 995840 | tf_op jit(solution)/shard_map/jit(_take)/gather | solution.py:220
  341.6 2.6 copy.2751
  347.5 2.8 copy.2769
  350.3 2.5 gather_fusion.5
  357.7 2.6 copy.2766
  360.3 2.5 gather_fusion.4
  368.7 4.9 %subtract_multiply_fusion = f32[13,6,6,6,128]{4,0,2,1,3:T(8,128)S(1)} fusion(f32[13,6,6,128]{3,0,2,1:T(8,128)S(1)} %add_multiply_fusion.1, f32[6,128]{1,0:T(8,128)S(1)} %copy-done.114, f32[13,6,6,128]{3,0,2,1:T(8,128)S(1)} %add_multiply_fusion.2, f32[6,128]{1,0:T(8,128)} %copy-done.115, f32[13,6,6,128]{3,0,2,1:T(8,128)S(1)} %copy-done.7, ...), kind=kLoop, calls=%fused_computation.16 | loop fusion | flops 18330624 | bytes 8761344 | tf_op jit(solution)/shard_map/mul | solution.py:234
  (578 shorter events, 80.1 us)
Async XLA Ops:
  2.3 37.0 %all-to-all-start.1 = ((f32[1,1,128]{1,0,2:T(1,128)}), f32[1,1,128]{1,0,2:T(1,128)S(1)}, u32[]{:S(2)}, u32[]{:S(2)}) async-start(f32[1,1,128]{1,0,2:T(1,128)} %copy.2597), calls=%async_computation.1 | async-start | bytes 131072 | tf_op jit(solution)/shard_map/all_to_all | solution.py:266
  28.3 22.8 %copy-start.152 = (f32[5,6,6]{0,2,1:T(8,128)S(1)}, f32[5,6,6]{0,2,1:T(8,128)}, u32[]{:S(2)}) copy-start(f32[5,6,6]{0,2,1:T(8,128)} %constant.79.clone) | copy-start | bytes 2164
  28.3 27.9 %copy-start.154 = (f32[5,6]{1,0:T(8,128)S(1)}, f32[5,6]{1,0:T(8,128)}, u32[]{:S(2)}) copy-start(f32[5,6]{1,0:T(8,128)} %constant.77.clone) | copy-start | bytes 364
  28.3 28.1 %copy-start.153 = (f32[5,6]{1,0:T(8,128)S(1)}, f32[5,6]{1,0:T(8,128)}, u32[]{:S(2)}) copy-start(f32[5,6]{1,0:T(8,128)} %constant.78.clone) | copy-start | bytes 364
  28.3 28.3 %copy-start.151 = (f32[5,6,6]{0,2,1:T(8,128)S(1)}, f32[5,6,6]{0,2,1:T(8,128)}, u32[]{:S(2)}) copy-start(f32[5,6,6]{0,2,1:T(8,128)} %constant.76.clone) | copy-start | bytes 2164
  28.3 30.4 %copy-start.150 = (f32[6]{0:T(128)S(1)}, f32[6]{0:T(128)}, u32[]{:S(2)}) copy-start(f32[6]{0:T(128)} %constant.80.clone) | copy-start | bytes 76
  39.3 111.5 %all-to-all-start = ((f32[13,216,128]{1,0,2:T(8,128)}), f32[13,216,128]{1,0,2:T(8,128)S(1)}, u32[]{:S(2)}, u32[]{:S(2)}) async-start(f32[13,216,128]{1,0,2:T(8,128)} %copy.2595), calls=%async_computation | async-start | bytes 4194304 | tf_op jit(solution)/shard_map/all_to_all | solution.py:265
  49.7 11.6 %copy-start.62 = (f32[6,128]{1,0:T(8,128)}, f32[6,128]{1,0:T(8,128)S(1)}, u32[]{:S(2)}) copy-start(f32[6,128]{1,0:T(8,128)S(1)} %get-tuple-element.390) | copy-start | bytes 9220
  49.7 11.6 %copy-start.113 = (f32[6,128]{1,0:T(8,128)}, f32[6,128]{1,0:T(8,128)S(1)}, u32[]{:S(2)}) copy-start(f32[6,128]{1,0:T(8,128)S(1)} %get-tuple-element.389) | copy-start | bytes 9220
  49.7 11.6 %copy-start.115 = (f32[6,128]{1,0:T(8,128)}, f32[6,128]{1,0:T(8,128)S(1)}, u32[]{:S(2)}) copy-start(f32[6,128]{1,0:T(8,128)S(1)} %get-tuple-element.392) | copy-start | bytes 9220
  49.7 11.6 %copy-start.41 = (f32[6,6,128]{2,1,0:T(8,128)}, f32[6,6,128]{2,1,0:T(8,128)S(1)}, u32[]{:S(2)}) copy-start(f32[6,6,128]{2,1,0:T(8,128)S(1)} %broadcast_multiply_fusion.2) | copy-start | bytes 55300
  51.4 10.0 %copy-start.70 = (f32[6,128]{1,0:T(8,128)}, f32[6,128]{1,0:T(8,128)S(1)}, u32[]{:S(2)}) copy-start(f32[6,128]{1,0:T(8,128)S(1)} %get-tuple-element.399) | copy-start | bytes 9220
  52.6 8.8 %copy-start.74 = (f32[6,128]{1,0:T(8,128)}, f32[6,128]{1,0:T(8,128)S(1)}, u32[]{:S(2)}) copy-start(f32[6,128]{1,0:T(8,128)S(1)} %get-tuple-element.397) | copy-start | bytes 9220
  52.6 8.8 %copy-start.76 = (f32[6,128]{1,0:T(8,128)}, f32[6,128]{1,0:T(8,128)S(1)}, u32[]{:S(2)}) copy-start(f32[6,128]{1,0:T(8,128)S(1)} %get-tuple-element.398) | copy-start | bytes 9220
  53.8 7.6 %copy-start.78 = (f32[6,128]{1,0:T(8,128)}, f32[6,128]{1,0:T(8,128)S(1)}, u32[]{:S(2)}) copy-start(f32[6,128]{1,0:T(8,128)S(1)} %get-tuple-element.395) | copy-start | bytes 9220
  53.8 7.6 %copy-start.80 = (f32[6,128]{1,0:T(8,128)}, f32[6,128]{1,0:T(8,128)S(1)}, u32[]{:S(2)}) copy-start(f32[6,128]{1,0:T(8,128)S(1)} %get-tuple-element.396) | copy-start | bytes 9220
  162.1 8.9 %copy-start.134 = (f32[128]{0:T(128)}, f32[128]{0:T(128)S(1)}, u32[]{:S(2)}) copy-start(f32[128]{0:T(128)S(1)} %add_reduce_fusion.5) | copy-start | bytes 1540
  162.2 11.8 %copy-start.136 = (f32[128]{0:T(128)}, f32[128]{0:T(128)S(1)}, u32[]{:S(2)}) copy-start(f32[128]{0:T(128)S(1)} %add_reduce_fusion.4) | copy-start | bytes 1540
  162.3 14.6 %copy-start.138 = (f32[128]{0:T(128)}, f32[128]{0:T(128)S(1)}, u32[]{:S(2)}) copy-start(f32[128]{0:T(128)S(1)} %get-tuple-element.13) | copy-start | bytes 1540
  162.3 14.7 %copy-start.130 = (f32[128]{0:T(128)}, f32[128]{0:T(128)S(1)}, u32[]{:S(2)}) copy-start(f32[128]{0:T(128)S(1)} %get-tuple-element.12) | copy-start | bytes 1540
  162.4 14.6 %copy-start.140 = (f32[128]{0:T(128)}, f32[128]{0:T(128)S(1)}, u32[]{:S(2)}) copy-start(f32[128]{0:T(128)S(1)} %get-tuple-element.11) | copy-start | bytes 1540
  162.4 14.8 %copy-start.132 = (f32[128]{0:T(128)}, f32[128]{0:T(128)S(1)}, u32[]{:S(2)}) copy-start(f32[128]{0:T(128)S(1)} %get-tuple-element.10) | copy-start | bytes 1540
  169.7 8.0 %copy-start.22 = (f32[13,36,128]{2,1,0:T(8,128)}, f32[13,36,128]{2,1,0:T(8,128)S(1)}, u32[]{:S(2)}) copy-start(f32[13,36,128]{2,1,0:T(8,128)S(1)} %get-tuple-element.317) | copy-start | bytes 718852
  185.2 92.9 %collective-permute-start = (f32[27,6,36,16]{2,3,1,0:T(8,128)}, f32[27,6,36,16]{2,3,1,0:T(8,128)}, u32[]{:S(2)}, u32[]{:S(2)}) collective-permute-start(f32[27,6,36,16]{2,3,1,0:T(8,128)} %copy.2746), channel_id=1, source_target_pairs={{0,1},{1,2},{2,3},{3,4},{4,5},{5,6},{6,7},{7,8},{8,9},{9,10},{10,1... | collective-permute-start | bytes 1119752 | tf_op jit(solution)/shard_map/ppermute | solution.py:23
  187.6 18.9 %copy-start.128 = (f32[6,1,128]{2,1,0:T(1,128)S(1)}, f32[6,1,128]{2,1,0:T(1,128)}, u32[]{:S(2)}) copy-start(f32[6,1,128]{2,1,0:T(1,128)} %get-tuple-element.322) | copy-start | bytes 9220
  187.6 18.9 %copy-start.129 = (f32[6,1,128]{2,1,0:T(1,128)S(1)}, f32[6,1,128]{2,1,0:T(1,128)}, u32[]{:S(2)}) copy-start(f32[6,1,128]{2,1,0:T(1,128)} %get-tuple-element.327) | copy-start | bytes 9220
  187.6 18.9 %copy-start.111 = (pred[6,6,6,128]{3,2,1,0:T(8,128)(4,1)S(1)}, pred[6,6,6,128]{3,2,1,0:T(8,128)(4,1)}, u32[]{:S(2)}) copy-start(pred[6,6,6,128]{3,2,1,0:T(8,128)(4,1)} %multiply_compare_fusion) | copy-start | bytes 82948
  191.1 22.9 %copy-start.1 = (f32[13,6,6,6,128]{4,0,2,1,3:T(8,128)S(1)}, f32[13,6,6,6,128]{4,0,2,1,3:T(8,128)}, u32[]{:S(2)}) copy-start(f32[13,6,6,6,128]{4,0,2,1,3:T(8,128)} %copy-done) | copy-start | bytes 4313092
  191.1 91.0 %collective-permute-start.1 = (f32[27,6,36,16]{2,3,1,0:T(8,128)}, f32[27,6,36,16]{2,3,1,0:T(8,128)}, u32[]{:S(2)}, u32[]{:S(2)}) collective-permute-start(f32[27,6,36,16]{2,3,1,0:T(8,128)} %copy.2747), channel_id=1, source_target_pairs={{1,0},{2,1},{3,2},{4,3},{5,4},{6,5},{7,6},{8,7},{9,8},{10,9},{11,1... | collective-permute-start | bytes 1119752 | tf_op jit(solution)/shard_map/ppermute | solution.py:24
  296.7 7.2 %copy-start.146 = (pred[128]{0:T(512)(128)(4,1)S(1)}, pred[128]{0:T(512)(128)(4,1)}, u32[]{:S(2)}) copy-start(pred[128]{0:T(512)(128)(4,1)} %get-tuple-element.360) | copy-start | bytes 388
  310.2 7.2 %copy-start.145 = (pred[128]{0:T(512)(128)(4,1)S(1)}, pred[128]{0:T(512)(128)(4,1)}, u32[]{:S(2)}) copy-start(pred[128]{0:T(512)(128)(4,1)} %get-tuple-element.362) | copy-start | bytes 388
  325.0 7.2 %copy-start.144 = (pred[128]{0:T(512)(128)(4,1)S(1)}, pred[128]{0:T(512)(128)(4,1)}, u32[]{:S(2)}) copy-start(pred[128]{0:T(512)(128)(4,1)} %get-tuple-element.364) | copy-start | bytes 388
  (127 other events, 256.9 us)
where the time goes:
time: 383 us; the launch traced here: 377 us
  waiting for transfers between devices  163 us (43%)
  local copies, waits for them, and re-layouts  118 us (31%)
  other arithmetic  46.5 us (12%)
  starting transfers between devices  44.7 us (12%)
    all_to_all x1, waiting for transfers between devices, local(): lax.all_to_all(state_send, ('gy', 'gz'), split_axis=2, concat_axis=2, til...  89.4 us
    ppermute x1, waiting for transfers between devices, padded(): before = lax.ppermute(last, axis, up)  62.9 us
    gather x12, local copies, waits for them, and re-layouts, finish(): far_rows = jnp.take(extended[:, face ^ 1], links[face], axis=-1)  36.2 us
    all_to_all x1, starting transfers between devices, local(): lax.all_to_all(order_tags, ('gy', 'gz'), split_axis=2, concat_axis=2, til...  20.3 us
    squeeze x7, local copies, waits for them, and re-layouts, finish(): far_rows = jnp.take(extended[:, face ^ 1], links[face], axis=-1)  20.1 us
    unnamed x322, local copies, waits for them, and re-layouts  19.7 us
    ppermute x1, starting transfers between devices, padded(): after = lax.ppermute(initial, axis, down)  15.3 us
    mul x122, local copies, waits for them, and re-layouts, apply_along(): term = matrix[:, column, :].reshape(shape) * piece  13.3 us
  transfers between devices with their start and end apart: 4, of which 3 were waited for; matrix products, arithmetic and copies ran while one was open for 10% of the time, Pallas kernels for 0%

commit v1 on v0

--- a/solution.py
+++ b/solution.py
@@ -261,8 +261,17 @@
     )
     live_send = positions % capacity < per_slot
     order_tags = jnp.where(live_send, order_send, 0).astype(jnp.float32).reshape(1, 1, slot_count)
+    serve_quotas = lambda state: jnp.concatenate(
+        lax.all_to_all(
+            jnp.stack(jnp.split(state, lax.axis_size(("gy", "gz")), 2), 0),
+            ("gy", "gz"),
+            split_axis=0,
+            concat_axis=0,
+        ),
+        2,
+    )
     moved, tags_in = (
-        lax.all_to_all(state_send, ("gy", "gz"), split_axis=2, concat_axis=2, tiled=True),
+        serve_quotas(state_send),
         lax.all_to_all(order_tags, ("gy", "gz"), split_axis=2, concat_axis=2, tiled=True),
     )
     degree = tags_in.reshape(slot_count).astype(jnp.int32)

time: 383 us -> 567 us (1.48)
  local copies, waits for them, and re-layouts: 118 us -> 305 us
  waiting for transfers between devices: 163 us -> 146 us
  starting transfers between devices: 44.7 us -> 55.7 us
    another operation x0 -> x71, local copies, waits for them, and re-layouts: none -> 188 us  [the longest x70 180 us: local(): jnp.stack(jnp.split(state, lax.axis_size(('gy', 'gz')), 2), 0)]
    reshape x1, local copies, waits for them, and re-layouts: 0.19 us -> 13.3 us  [local(): jnp.concatenate(lax.all_to_all(jnp.stack(jnp.split(state, lax.axis_size((...]
    all_to_all x1, waiting for transfers between devices: 89.4 us -> 76.8 us  [local(): lax.all_to_all(jnp.stack(jnp.split(state, lax.axis_size(('gy', 'gz')), 2)...]
    all_to_all x1, waiting for transfers between devices: 11 us -> 0.01 us  [local(): lax.all_to_all(order_tags, ('gy', 'gz'), split_axis=2, concat_axis=2, til...]
    all_to_all x1, starting transfers between devices: 6.72 us -> 17.7 us  [local(): lax.all_to_all(jnp.stack(jnp.split(state, lax.axis_size(('gy', 'gz')), 2)...]
    unnamed x322 -> x325, local copies, waits for them, and re-layouts: 19.7 us -> 8.96 us
    ppermute x1, waiting for transfers between devices: 62.9 us -> 69.5 us  [padded(): before = lax.ppermute(last, axis, up)]
    mul x122 -> x124, local copies, waits for them, and re-layouts: 13.3 us -> 13 us  [apply_along(): term = matrix[:, column, :].reshape(shape) * piece]
  transfers between devices with their start and end apart: 4 -> 4, of which waited for: 3 -> 2; matrix products, arithmetic and copies ran while one was open for 10% -> 37% of each run, Pallas kernels for 0% -> 0%
where the time goes in v1:
time: 567 us; the launch traced here: 556 us
  local copies, waits for them, and re-layouts  305 us (54%)
  waiting for transfers between devices  146 us (26%)
  starting transfers between devices  55.7 us (10%)
  other arithmetic  44.8 us (8%)
    another operation x70, local copies, waits for them, and re-layouts, local(): jnp.stack(jnp.split(state, lax.axis_size(('gy', 'gz')), 2), 0)  180 us
    all_to_all x1, waiting for transfers between devices, local(): lax.all_to_all(jnp.stack(jnp.split(state, lax.axis_size(('gy', 'gz')), 2)...  76.8 us
    ppermute x1, waiting for transfers between devices, padded(): before = lax.ppermute(last, axis, up)  69.5 us
    gather x12, local copies, waits for them, and re-layouts, finish(): far_rows = jnp.take(extended[:, face ^ 1], links[face], axis=-1)  36.3 us
    all_to_all x1, starting transfers between devices, local(): lax.all_to_all(order_tags, ('gy', 'gz'), split_axis=2, concat_axis=2, til...  20.3 us
    squeeze x7, local copies, waits for them, and re-layouts, finish(): far_rows = jnp.take(extended[:, face ^ 1], links[face], axis=-1)  20.2 us
    all_to_all x1, starting transfers between devices, local(): lax.all_to_all(jnp.stack(jnp.split(state, lax.axis_size(('gy', 'gz')), 2)...  17.7 us
    ppermute x1, starting transfers between devices, padded(): after = lax.ppermute(initial, axis, down)  15.4 us
  transfers between devices with their start and end apart: 4, of which 2 were waited for; matrix products, arithmetic and copies ran while one was open for 37% of the time, Pallas kernels for 0%

profile of v1, /device:TPU:32, one launch (start us, length us, event | category | flops | bytes accessed | tf_op | source)
XLA Modules:
  0.0 556.2 jit_solution(15820753606866118021)
XLA Ops:
  2.3 20.3 %all-to-all-start.1 = ((f32[1,1,128]{1,0,2:T(1,128)}), f32[1,1,128]{1,0,2:T(1,128)S(1)}, u32[]{:S(2)}, u32[]{:S(2)}) async-start(f32[1,1,128]{1,0,2:T(1,128)} %copy.2794), calls=%async_computation.1 | async-start | bytes 131072 | tf_op jit(solution)/shard_map/all_to_all | solution.py:275
  22.6 20.1 %slice_bitcast_fusion.38 = (f32[1,13,216,2]{3,2,1,0:T(8,128)}, f32[1,13,216,2]{3,2,1,0:T(8,128)}, f32[1,13,216,2]{3,2,1,0:T(8,128)}, f32[1,13,216,2]{3,2,1,0:T(8...) fusion(f32[13,216,128]{2,1,0:T(8,128)} %param.11), kind=kLoop, calls=%fused_computation.58 | loop fusion | bytes 853632 | tf_op jit(solution)/shard_map/stack | solution.py:266
  42.7 12.9 %slice_bitcast_fusion.19 = (f32[1,13,216,2]{3,2,1,0:T(8,128)}, f32[1,13,216,2]{3,2,1,0:T(8,128)}, f32[1,13,216,2]{3,2,1,0:T(8,128)}, f32[1,13,216,2]{3,2,1,0:T(8...) fusion(f32[13,216,128]{2,1,0:T(8,128)S(1)} %copy-done), kind=kLoop, calls=%fused_computation.39 | loop fusion | bytes 853632 | tf_op jit(solution)/shard_map/stack | solution.py:266
  55.6 12.9 %slice_bitcast_fusion = (f32[1,13,216,2]{3,2,1,0:T(8,128)}, f32[1,13,216,2]{3,2,1,0:T(8,128)}, f32[1,13,216,2]{3,2,1,0:T(8,128)}, f32[1,13,216,2]{3,2,1,0:T(8,12...) fusion(f32[13,216,128]{2,1,0:T(8,128)S(1)} %copy-done), kind=kLoop, calls=%fused_computation.20 | loop fusion | bytes 853632 | tf_op jit(solution)/shard_map/stack | solution.py:266
  68.6 5.7 %slice_bitcast_fusion.57 = (f32[1,13,216,2]{3,2,1,0:T(8,128)S(1)}, f32[1,13,216,2]{3,2,1,0:T(8,128)}, f32[1,13,216,2]{3,2,1,0:T(8,128)}, f32[1,13,216,2]{3,2,1,0...) fusion(f32[13,216,128]{2,1,0:T(8,128)S(1)} %copy-done), kind=kLoop, calls=%fused_computation.77 | loop fusion | bytes 314496 | tf_op jit(solution)/shard_map/stack | solution.py:266
  195.0 7.6 %stack.280 = f32[64,13,216,2]{2,0,3,1:T(8,128)S(1)} concatenate(f32[1,13,216,2]{2,0,3,1:T(1,128)} %copy.3093, f32[1,13,216,2]{2,0,3,1:T(1,128)} %copy.3094, f32[1,13,216,2]{2,0,3,1:T(1,128)} %copy.3095, f32[1,13,216,2]{2,0,3,1:T(1,128)} %copy.3096, f32[1,13,216,2]{2,0,3,1:T(1,128)} %copy.3097, f32[1,13,216,2]{2,0,3,1:T(1,128)} %copy.3098, f32[1,13,216,2]{2,0,3,1:T(1,128)} %copy.3099, ...), dimensions={0} | concatenate | bytes 2875392 | tf_op jit(solution)/shard_map/stack | solution.py:266
  205.2 17.7 %all-to-all-start = ((f32[64,13,216,2]{2,3,1,0:T(2,128)}), f32[64,13,216,2]{2,3,1,0:T(2,128)S(1)}, u32[]{:S(2)}, u32[]{:S(2)}) async-start(f32[64,13,216,2]{2,3,1,0:T(2,128)} %copy.2792), calls=%async_computation | async-start | bytes 3407872 | tf_op jit(solution)/shard_map/all_to_all | solution.py:265
  234.2 76.8 %all-to-all-done = f32[64,13,216,2]{2,3,1,0:T(2,128)S(1)} async-done(((f32[64,13,216,2]{2,3,1,0:T(2,128)}), f32[64,13,216,2]{2,3,1,0:T(2,128)S(1)}, u32[]{:S(2)}, u32[]{:S(2)}) %all-to-all-start) | async-done | bytes 1437728 | tf_op jit(solution)/shard_map/all_to_all | solution.py:265
  310.9 13.3 %copy.2793 = f32[13,216,64,2]{0,3,2,1:T(2,128)} copy(f32[13,216,64,2]{1,3,0,2:T(2,128)S(1)} %bitcast.1250) | data formatting | bytes 2875392 | tf_op jit(solution)/shard_map/reshape | solution.py:264
  324.2 8.4 %copy.2796 = f32[13,6,6,6,128]{4,0,2,1,3:T(8,128)S(1)} copy(f32[13,6,6,6,128]{0,4,3,2,1:T(8,128)} %bitcast.1249) | data formatting | bytes 2875392 | tf_op jit(solution)/shard_map/reshape;reshape | solution.py:159
  355.8 3.9 fusion.164
  359.7 3.6 copy.2943
  365.6 3.5 copy.2944
  369.1 15.4 %collective-permute-start.1 = (f32[27,6,36,16]{2,3,1,0:T(8,128)}, f32[27,6,36,16]{2,3,1,0:T(8,128)}, u32[]{:S(2)}, u32[]{:S(2)}) collective-permute-start(f32[27,6,36,16]{2,3,1,0:T(8,128)} %copy.2944), channel_id=1, source_target_pairs={{1,0},{2,1},{3,2},{4,3},{5,4},{6,5},{7,6},{8,7},{9,8},{10,9},{11,1... | collective-permute-start | bytes 1119752 | tf_op jit(solution)/shard_map/ppermute | solution.py:24
  384.5 2.7 slice_bitcast_fusion.92
  388.4 69.5 %collective-permute-done = f32[27,6,36,16]{2,3,1,0:T(8,128)} collective-permute-done((f32[27,6,36,16]{2,3,1,0:T(8,128)}, f32[27,6,36,16]{2,3,1,0:T(8,128)}, u32[]{:S(2)}, u32[]{:S(2)}) %collective-permute-start) | collective-permute-done | bytes 373280 | tf_op jit(solution)/shard_map/ppermute | solution.py:23
  457.9 4.0 copy.2945
  461.9 3.6 copy.2946
  465.5 5.6 %pad_maximum_fusion = f32[27,6,36,160]{3,2,0,1:T(8,128)S(1)} fusion(f32[27,6,36,16]{3,2,0,1:T(8,128)} %copy.2946, f32[27,6,36,128]{3,2,0,1:T(8,128)S(1)} %fusion.5, f32[27,6,36,16]{3,2,0,1:T(8,128)} %copy.2945), kind=kLoop, calls=%fused_computation.6 | loop fusion | flops 1866240 | bytes 7464960 | tf_op jit(solution)/shard_map/concatenate | solution.py:25
  473.1 3.4 copy.2959
  476.5 3.9 gather_fusion.3
  480.4 3.3 copy.2960
  486.7 3.4 copy.2955
  490.2 3.9 gather_fusion.2
  494.0 3.3 copy.2956
  501.6 3.4 copy.2951
  505.0 3.9 gather_fusion.1
  508.9 3.3 copy.2952
  515.2 2.6 copy.2947
  517.8 3.9 gather_fusion
  527.7 2.8 copy.2966
  548.2 4.4 subtract_multiply_fusion
  (649 shorter events, 199.8 us)
Async XLA Ops:
  2.3 202.9 %all-to-all-start.1 = ((f32[1,1,128]{1,0,2:T(1,128)}), f32[1,1,128]{1,0,2:T(1,128)S(1)}, u32[]{:S(2)}, u32[]{:S(2)}) async-start(f32[1,1,128]{1,0,2:T(1,128)} %copy.2794), calls=%async_computation.1 | async-start | bytes 131072 | tf_op jit(solution)/shard_map/all_to_all | solution.py:275
  22.6 20.2 %copy-start = (f32[13,216,128]{2,1,0:T(8,128)S(1)}, f32[13,216,128]{2,1,0:T(8,128)}, u32[]{:S(2)}) copy-start(f32[13,216,128]{2,1,0:T(8,128)} %param.11) | copy-start | bytes 4313092
  105.5 5.1 copy-start.19
  130.2 5.1 copy-start.15
  149.0 6.9 %copy-start.12 = (f32[1,13,216,2]{3,2,1,0:T(8,128)S(1)}, f32[1,13,216,2]{3,2,1,0:T(8,128)}, u32[]{:S(2)}) copy-start(f32[1,13,216,2]{3,2,1,0:T(8,128)} %get-tuple-element.89) | copy-start | bytes 67396
  163.1 5.0 copy-start.10
  187.8 5.1 copy-start.6
  205.2 17.8 %copy-start.152 = (s32[128]{0:T(128)S(1)}, s32[128]{0:T(128)}, u32[]{:S(2)}) copy-start(s32[128]{0:T(128)} %get-tuple-element.438) | copy-start | bytes 1540
  205.2 21.3 %copy-start.154 = (pred[6]{0:T(512)(128)(4,1)S(1)}, pred[6]{0:T(512)(128)(4,1)}, u32[]{:S(2)}) copy-start(pred[6]{0:T(512)(128)(4,1)} %iota_compare_fusion.3) | copy-start | bytes 22
  205.2 22.2 %copy-start.156 = (f32[5,6,6]{0,2,1:T(8,128)S(1)}, f32[5,6,6]{0,2,1:T(8,128)}, u32[]{:S(2)}) copy-start(f32[5,6,6]{0,2,1:T(8,128)} %constant.79.clone) | copy-start | bytes 2164
  205.2 23.9 %copy-start.158 = (f32[5,6]{1,0:T(8,128)S(1)}, f32[5,6]{1,0:T(8,128)}, u32[]{:S(2)}) copy-start(f32[5,6]{1,0:T(8,128)} %constant.77.clone) | copy-start | bytes 364
  205.2 24.1 %copy-start.157 = (f32[5,6]{1,0:T(8,128)S(1)}, f32[5,6]{1,0:T(8,128)}, u32[]{:S(2)}) copy-start(f32[5,6]{1,0:T(8,128)} %constant.78.clone) | copy-start | bytes 364
  205.2 105.7 %all-to-all-start = ((f32[64,13,216,2]{2,3,1,0:T(2,128)}), f32[64,13,216,2]{2,3,1,0:T(2,128)S(1)}, u32[]{:S(2)}, u32[]{:S(2)}) async-start(f32[64,13,216,2]{2,3,1,0:T(2,128)} %copy.2792), calls=%async_computation | async-start | bytes 3407872 | tf_op jit(solution)/shard_map/all_to_all | solution.py:265
  222.9 7.2 %copy-start.155 = (f32[5,6,6]{0,2,1:T(8,128)S(1)}, f32[5,6,6]{0,2,1:T(8,128)}, u32[]{:S(2)}) copy-start(f32[5,6,6]{0,2,1:T(8,128)} %constant.76.clone) | copy-start | bytes 2164
  222.9 9.3 %copy-start.153 = (f32[6]{0:T(128)S(1)}, f32[6]{0:T(128)}, u32[]{:S(2)}) copy-start(f32[6]{0:T(128)} %constant.80.clone) | copy-start | bytes 76
  226.6 97.6 %copy-start.120 = (f32[6,128]{1,0:T(8,128)}, f32[6,128]{1,0:T(8,128)S(1)}, u32[]{:S(2)}) copy-start(f32[6,128]{1,0:T(8,128)S(1)} %get-tuple-element.461) | copy-start | bytes 9220
  226.6 97.6 %copy-start.121 = (f32[6,128]{1,0:T(8,128)}, f32[6,128]{1,0:T(8,128)S(1)}, u32[]{:S(2)}) copy-start(f32[6,128]{1,0:T(8,128)S(1)} %get-tuple-element.463) | copy-start | bytes 9220
  228.3 119.5 %copy-start.64 = (f32[36,128]{1,0:T(8,128)}, f32[36,128]{1,0:T(8,128)S(1)}, u32[]{:S(2)}) copy-start(f32[36,128]{1,0:T(8,128)S(1)} %mul.5151) | copy-start | bytes 55300
  228.4 119.5 %copy-start.66 = (f32[36,128]{1,0:T(8,128)}, f32[36,128]{1,0:T(8,128)S(1)}, u32[]{:S(2)}) copy-start(f32[36,128]{1,0:T(8,128)S(1)} %mul.5158) | copy-start | bytes 55300
  341.1 10.9 %copy-start.136 = (f32[128]{0:T(128)}, f32[128]{0:T(128)S(1)}, u32[]{:S(2)}) copy-start(f32[128]{0:T(128)S(1)} %get-tuple-element.13) | copy-start | bytes 1540
  341.1 13.9 %copy-start.140 = (f32[128]{0:T(128)}, f32[128]{0:T(128)S(1)}, u32[]{:S(2)}) copy-start(f32[128]{0:T(128)S(1)} %get-tuple-element.12) | copy-start | bytes 1540
  341.2 7.6 %copy-start.134 = (f32[128]{0:T(128)}, f32[128]{0:T(128)S(1)}, u32[]{:S(2)}) copy-start(f32[128]{0:T(128)S(1)} %get-tuple-element.15) | copy-start | bytes 1540
  341.2 13.7 %copy-start.138 = (f32[128]{0:T(128)}, f32[128]{0:T(128)S(1)}, u32[]{:S(2)}) copy-start(f32[128]{0:T(128)S(1)} %get-tuple-element.14) | copy-start | bytes 1540
  347.5 8.2 %copy-start.31 = (f32[13,36,128]{2,1,0:T(8,128)}, f32[13,36,128]{2,1,0:T(8,128)S(1)}, u32[]{:S(2)}) copy-start(f32[13,36,128]{2,1,0:T(8,128)S(1)} %get-tuple-element.388) | copy-start | bytes 718852
  348.8 7.0 %copy-start.32 = (f32[13,36,128]{2,1,0:T(8,128)}, f32[13,36,128]{2,1,0:T(8,128)S(1)}, u32[]{:S(2)}) copy-start(f32[13,36,128]{2,1,0:T(8,128)S(1)} %get-tuple-element.377) | copy-start | bytes 718852
  363.2 94.7 %collective-permute-start = (f32[27,6,36,16]{2,3,1,0:T(8,128)}, f32[27,6,36,16]{2,3,1,0:T(8,128)}, u32[]{:S(2)}, u32[]{:S(2)}) collective-permute-start(f32[27,6,36,16]{2,3,1,0:T(8,128)} %copy.2943), channel_id=1, source_target_pairs={{0,1},{1,2},{2,3},{3,4},{4,5},{5,6},{6,7},{7,8},{8,9},{9,10},{10,1... | collective-permute-start | bytes 1119752 | tf_op jit(solution)/shard_map/ppermute | solution.py:23
  369.1 18.1 %copy-start.2 = (f32[13,6,6,6,128]{4,0,2,3,1:T(8,128)S(1)}, f32[13,6,6,6,128]{4,0,2,3,1:T(8,128)}, u32[]{:S(2)}) copy-start(f32[13,6,6,6,128]{4,0,2,3,1:T(8,128)} %copy-done.1) | copy-start | bytes 4313092
  369.1 92.9 %collective-permute-start.1 = (f32[27,6,36,16]{2,3,1,0:T(8,128)}, f32[27,6,36,16]{2,3,1,0:T(8,128)}, u32[]{:S(2)}, u32[]{:S(2)}) collective-permute-start(f32[27,6,36,16]{2,3,1,0:T(8,128)} %copy.2944), channel_id=1, source_target_pairs={{1,0},{2,1},{3,2},{4,3},{5,4},{6,5},{7,6},{8,7},{9,8},{10,9},{11,1... | collective-permute-start | bytes 1119752 | tf_op jit(solution)/shard_map/ppermute | solution.py:24
  476.5 7.2 %copy-start.148 = (pred[128]{0:T(512)(128)(4,1)S(1)}, pred[128]{0:T(512)(128)(4,1)}, u32[]{:S(2)}) copy-start(pred[128]{0:T(512)(128)(4,1)} %get-tuple-element.429) | copy-start | bytes 388
  490.2 7.2 %copy-start.147 = (pred[128]{0:T(512)(128)(4,1)S(1)}, pred[128]{0:T(512)(128)(4,1)}, u32[]{:S(2)}) copy-start(pred[128]{0:T(512)(128)(4,1)} %get-tuple-element.431) | copy-start | bytes 388
  505.0 7.2 %copy-start.146 = (pred[128]{0:T(512)(128)(4,1)S(1)}, pred[128]{0:T(512)(128)(4,1)}, u32[]{:S(2)}) copy-start(pred[128]{0:T(512)(128)(4,1)} %get-tuple-element.433) | copy-start | bytes 388
  517.8 6.5 %copy-start.145 = (pred[128]{0:T(512)(128)(4,1)S(1)}, pred[128]{0:T(512)(128)(4,1)}, u32[]{:S(2)}) copy-start(pred[128]{0:T(512)(128)(4,1)} %get-tuple-element.16) | copy-start | bytes 388
  (131 other events, 287.5 us)
